TPU v7x, 32 devices: a whole 2x2x4 slice. The times are simulated.
32 devices in a mesh: kv: 2 (over x), seq: 16 (over z, y, core).
Axes of the slice: x: 2, y: 2, z: 4, core: 2. Of those that a mesh axis runs over, the one named last changes fastest.
Arguments:
- hidden: bfloat16 [1024, 2048], P('seq', 'kv'), may hold values from -1.5 to 1.5
- in_gain: float32 [2048], replicated, may hold values from 0.5 to 1.5
- w_query: bfloat16 [2048, 2048], P(None, 'kv'), may hold values from -0.125 to 0.125
- key_projection_weight: bfloat16 [2048, 1024], P(None, 'kv'), may hold values from -0.125 to 0.125
- value_projection_weight: bfloat16 [2048, 1024], P(None, 'kv'), may hold values from -0.125 to 0.125
- w_gate: bfloat16 [2048, 16], P(None, 'kv'), may hold values from -0.125 to 0.125
- w_out: bfloat16 [2048, 2048], P('kv'), may hold values from -0.125 to 0.125
- q_gain: float32 [128], replicated, may hold values from 0.1 to 1.9
- k_gain: float32 [128], replicated, may hold values from 0.1 to 1.9
- cache_keys: bfloat16 [32768, 8, 128], P('seq', 'kv'), may hold values from -160 to 160
- pooled_cache_values: bfloat16 [32768, 8, 128], P('seq', 'kv'), may hold values from -6 to 6
- prefix_len: int32 [4], replicated, may hold values from 1024 to 8192, as said below
- own_len: int32 [32], replicated, may hold values from 256 to 2048, as said below
- request_group: int32 [32], replicated, may hold values from 0 to 3, as said below
- parents: int32 [32, 32], P('seq'), may hold values from 0 to 30, as said below
- accepted_leaf: int32 [32], P('seq'), may hold values from 0 to 31
Outputs:
- layer_out: bfloat16 [1024, 2048], P('seq', 'kv')
- accepted_keys: bfloat16 [32, 32, 1024], P('seq', None, 'kv')
- accepted_values: bfloat16 [32, 32, 1024], P('seq', None, 'kv')
Inputs may be any that keep to these rules, and one draw needn't show every extreme that they name: parents[r, 0] is 0 and node 0 is the root; for i >= 1, parents[r, i] < i. `prefix_len`: the lengths sum to 32768 // 2; one is exactly 8192 and one exactly 1024. `own_len`: the lengths sum to 32768 // 2; one is exactly 2048 and one exactly 256. `request_group`: every group holds exactly 8 requests.
All inputs are finite; a program needn't handle non-finite values.
Results may differ from a plain program's by a relative error of at most 0.017.
The roundings to bfloat16 on the way count: a program that leaves them out, or rounds other values in their place, can miss the bound.
Values may be sent and summed in bfloat16 or wider, within the bound.
A program may use at most 128 MiB of HBM per device.

v0:
```python
import functools
import math

import jax
import jax.numpy as jnp
from jax import lax
from jax.experimental import pallas as pl
from jax.experimental.pallas import tpu as pltpu
from jax.sharding import PartitionSpec as P

EPSILON = 1e-06
ROPE_BASE = 1000000.0
NEGATIVE = -1e30


def rms_scale(values, scales):
    mean_square = jnp.mean(values * values, axis=-1, keepdims=True)
    return values * lax.rsqrt(mean_square + EPSILON) * scales


def rope_tables(positions, head_width):
    half_width = head_width // 2
    freqs = jnp.exp(
        jnp.arange(half_width, dtype=jnp.float32) * (-2.0 * math.log(ROPE_BASE) / head_width)
    )
    angles = positions[:, None] * freqs[None, :]
    cosine = jnp.cos(angles)
    sine = jnp.sin(angles)
    return (
        jnp.concatenate([cosine, cosine], axis=-1),
        jnp.concatenate([-sine, sine], axis=-1),
    )


def tree_paths(parents):
    width = parents.shape[-1]
    nodes = jnp.arange(width, dtype=jnp.int32)
    linked = (parents[:, :, None] == nodes[None, None, :]).astype(jnp.float32)
    identity_mat = jnp.eye(width, dtype=jnp.float32)
    reach = jnp.minimum(identity_mat[None] + linked * (1.0 - identity_mat[None]), 1.0)
    for squaring in range(max(1, (width - 1).bit_length())):
        reach = jnp.minimum(
            jnp.einsum("mij,mjk->mik", reach, reach, precision=lax.Precision.HIGHEST), 1.0
        )
    depth_f = jnp.sum(reach, axis=-1) - 1.0
    return (reach, depth_f)


def accepted_rows(reach, depth_f, leaves, tree_rows):
    width = reach.shape[-1]
    nodes = jnp.arange(width, dtype=jnp.int32)
    leaf_pick = (leaves[:, None] == nodes[None, :]).astype(jnp.float32)
    on_path = jnp.einsum("mi,mij->mj", leaf_pick, reach, precision=lax.Precision.HIGHEST)
    levels = (depth_f[:, None, :] == nodes.astype(jnp.float32)[None, :, None]).astype(jnp.float32)
    select = levels * on_path[:, None, :]
    return jnp.einsum(
        "mdj,mjc->mdc", select, tree_rows.astype(jnp.float32), precision=lax.Precision.HIGHEST
    ).astype(jnp.bfloat16)


def lowest(distance):
    return distance & -distance


def flip(index, distance):
    out = index
    bit = 1
    while bit <= distance:
        if distance & bit:
            out = out + bit * (1 - 2 * ((index // bit) % 2))
        bit *= 2
    return out


def one_bits(count):
    bits = []
    bit = 1
    while bit < count:
        bits.append(bit)
        bit *= 2
    return bits


def greet(me, count, kv, kv_count):
    barrier = pltpu.get_barrier_semaphore()
    bits = one_bits(count)
    for bit in bits:
        pl.semaphore_signal(barrier, inc=1, device_id={"seq": flip(me, bit)})
    for hop in range(1, kv_count):
        pl.semaphore_signal(barrier, inc=1, device_id={"kv": (kv + hop) % kv_count})
    pl.semaphore_wait(barrier, len(bits) + kv_count - 1)


def layer_kernel(
    count,
    kv_count,
    score_scale,
    hidden_ref,
    in_gain_ref,
    w_query_ref,
    w_key_ref,
    w_value_ref,
    w_gate_ref,
    q_gain_ref,
    k_gain_ref,
    cos_ref,
    sin_ref,
    seen_ref,
    all_ref,
    key_ref,
    value_ref,
    tree_ref,
    tree_lse_ref,
    gate_ref,
    wide,
    w_query,
    w_key,
    w_value,
    w_gate,
    in_gain,
    q_gain,
    k_gain,
    load_sem,
    wide_send,
    wide_recv,
    send_sem,
    recv_sem,
):
    me = lax.axis_index("seq")
    kv = lax.axis_index("kv")
    loads = [
        pltpu.make_async_copy(source, target, load_sem.at[which])
        for which, (source, target) in enumerate(
            [
                (hidden_ref, wide.at[kv]),
                (in_gain_ref, in_gain),
                (q_gain_ref, q_gain),
                (k_gain_ref, k_gain),
                (w_query_ref, w_query),
                (w_key_ref, w_key),
                (w_value_ref, w_value),
                (w_gate_ref, w_gate),
            ]
        )
    ]
    for load in loads:
        load.start()
    loads[0].wait()
    greet(me, count, kv, kv_count)

    def wide_message(hop, owner):
        return pltpu.make_async_remote_copy(
            src_ref=wide.at[owner],
            dst_ref=wide.at[owner],
            send_sem=wide_send.at[hop],
            recv_sem=wide_recv.at[hop],
            device_id={"kv": (kv + hop) % kv_count},
        )

    wide_sent = [wide_message(hop, kv) for hop in range(1, kv_count)]
    for copy in wide_sent:
        copy.start()
    for hop in range(1, kv_count):
        wide_message(hop, (kv + kv_count - hop) % kv_count).wait_recv()
    rows = jnp.concatenate([wide[at] for at in range(kv_count)], axis=1).astype(jnp.float32)
    for load in loads[1:4]:
        load.wait()
    normed = rms_scale(rows, in_gain[...]).astype(jnp.bfloat16)

    def rotated(values, gain):
        values = rms_scale(values, gain[...])
        return (values * cos_ref[...] + pltpu.roll(values, 64, 1) * sin_ref[...]).astype(jnp.bfloat16)

    loads[4].wait()
    query = jnp.dot(normed, w_query[...], preferred_element_type=jnp.float32)
    heads = query.shape[1] // 128
    queries = [rotated(query[:, h * 128 : (h + 1) * 128], q_gain) for h in range(heads)]
    for head in range(heads):
        all_ref[me, :, head * 128 : (head + 1) * 128] = queries[head]

    def message(distance, owner):
        return pltpu.make_async_remote_copy(
            src_ref=all_ref.at[owner],
            dst_ref=all_ref.at[owner],
            send_sem=send_sem.at[distance],
            recv_sem=recv_sem.at[distance],
            device_id={"seq": flip(me, lowest(distance))},
        )

    sent = []

    def hand_on(distance):
        owner = flip(me, distance)
        if distance:
            message(distance, owner).wait_recv()
        for bit in reversed(one_bits(lowest(distance) if distance else count)):
            copy = message(distance | bit, owner)
            copy.start()
            sent.append(copy)

    hand_on(0)
    local_kv = key_ref.shape[1] // 128
    per_kv = heads // local_kv
    tokens = hidden_ref.shape[0]

    def keys_work():
        loads[5].wait()
        key = jnp.dot(normed, w_key[...], preferred_element_type=jnp.float32)
        for at in range(local_kv):
            cols = slice(at * 128, (at + 1) * 128)
            key_ref[:, cols] = rotated(key[:, cols], k_gain)

    def values_work():
        loads[6].wait()
        loads[7].wait()
        value_ref[...] = jnp.dot(
            normed, w_value[...], preferred_element_type=jnp.float32
        ).astype(jnp.bfloat16)
        gate_ref[...] = jax.nn.sigmoid(
            lax.dot_general(
                normed, w_gate[...], (((1,), (1,)), ((), ())), preferred_element_type=jnp.float32
            )
        )
        tree_lse_ref[...] = jnp.zeros(tree_lse_ref.shape, jnp.float32)

    def tree_work(at):
        cols = slice(at * 128, (at + 1) * 128)
        stacked = jnp.concatenate(queries[at * per_kv : (at + 1) * per_kv], axis=0)
        scores = (
            lax.dot_general(
                stacked,
                key_ref[:, cols],
                (((1,), (1,)), ((), ())),
                preferred_element_type=jnp.float32,
            )
            * score_scale
        )
        seen = jnp.concatenate([seen_ref[...]] * per_kv, axis=0) > 0.5
        scores = jnp.where(seen, scores, NEGATIVE)
        top = jnp.max(scores, axis=1, keepdims=True)
        weights = jnp.where(seen, jnp.exp(scores - top), 0.0)
        total = jnp.sum(weights, axis=1, keepdims=True)
        mixed = (
            jnp.dot(
                weights.astype(jnp.bfloat16), value_ref[:, cols], preferred_element_type=jnp.float32
            )
            / total
        )
        lse = top + jnp.log(total)
        for sub in range(per_kv):
            head = at * per_kv + sub
            part = slice(sub * tokens, (sub + 1) * tokens)
            tree_ref[:, head * 128 : (head + 1) * 128] = mixed[part]
            tree_lse_ref[:, head : head + 1] = lse[part]

    work = [keys_work, values_work] + [functools.partial(tree_work, at) for at in range(local_kv)]
    order = sorted(range(2, count, 2), key=lambda d: (-lowest(d), d))
    for distance in order:
        if work:
            work.pop(0)()
        hand_on(distance)
    for rest in work:
        rest()
    for distance in range(1, count, 2):
        hand_on(distance)
    for copy in wide_sent + sent:
        copy.wait_send()


def layer_front(
    hidden, in_gain, w_query, w_key, w_value, w_gate, q_gain, k_gain, cosine, sine, seen, count, kv_count, score_scale
):
    tokens = hidden.shape[0]
    width = w_query.shape[1]
    vmem = pl.BlockSpec(memory_space=pltpu.VMEM)
    hbm = pl.BlockSpec(memory_space=pltpu.HBM)
    return pl.pallas_call(
        functools.partial(layer_kernel, count, kv_count, score_scale),
        out_shape=(
            jax.ShapeDtypeStruct((count, tokens, width), jnp.bfloat16),
            jax.ShapeDtypeStruct((tokens, w_key.shape[1]), jnp.bfloat16),
            jax.ShapeDtypeStruct((tokens, w_value.shape[1]), jnp.bfloat16),
            jax.ShapeDtypeStruct((tokens, width), jnp.float32),
            jax.ShapeDtypeStruct((tokens, 128), jnp.float32),
            jax.ShapeDtypeStruct((tokens, w_gate.shape[0]), jnp.float32),
        ),
        in_specs=[hbm] * 8 + [vmem] * 3,
        out_specs=(vmem,) * 6,
        scratch_shapes=[
            pltpu.VMEM((kv_count,) + hidden.shape, hidden.dtype),
            pltpu.VMEM(w_query.shape, w_query.dtype),
            pltpu.VMEM(w_key.shape, w_key.dtype),
            pltpu.VMEM(w_value.shape, w_value.dtype),
            pltpu.VMEM(w_gate.shape, w_gate.dtype),
            pltpu.VMEM((1, in_gain.shape[0]), jnp.float32),
            pltpu.VMEM((1, 128), jnp.float32),
            pltpu.VMEM((1, 128), jnp.float32),
            pltpu.SemaphoreType.DMA((8,)),
            pltpu.SemaphoreType.DMA((kv_count,)),
            pltpu.SemaphoreType.DMA((kv_count,)),
            pltpu.SemaphoreType.DMA((count,)),
            pltpu.SemaphoreType.DMA((count,)),
        ],
        compiler_params=pltpu.CompilerParams(
            collective_id=0, has_side_effects=True, vmem_limit_bytes=60 * 2**20
        ),
        name="layer_front",
    )(hidden, in_gain[None], w_query, w_key, w_value, w_gate, q_gain[None], k_gain[None], cosine, sine, seen)


def merge_kernel(
    count,
    kv_count,
    part_ref,
    lse_ref,
    tree_ref,
    tree_lse_ref,
    gate_ref,
    w_out_ref,
    hidden_ref,
    out_ref,
    got,
    got_lse,
    mine_lse,
    held,
    held_lse,
    w_out,
    attended,
    outgoing,
    arrived,
    send_sem,
    recv_sem,
    load_sem,
    out_send,
    out_recv,
):
    me = lax.axis_index("seq")
    kv = lax.axis_index("kv")
    heads = part_ref.shape[2] // 128
    load = pltpu.make_async_copy(w_out_ref, w_out, load_sem)
    load.start()
    rows = part_ref.shape[1]

    def across(level):
        turned = jnp.transpose(level)[:8]
        return jnp.concatenate([turned] * (128 // rows), axis=1)

    for distance in range(count):
        mine_lse[distance] = across(lse_ref[flip(me, distance)])
    greet(me, count, kv, kv_count)

    def messages(distance):
        owner = flip(me, distance)
        if distance % 2:
            sources = (part_ref.at[owner], mine_lse.at[distance])
        else:
            sources = (held.at[distance // 2], held_lse.at[distance // 2])
        return [
            pltpu.make_async_remote_copy(
                src_ref=source,
                dst_ref=target.at[distance],
                send_sem=send_sem.at[which, distance],
                recv_sem=recv_sem.at[which, distance],
                device_id={"seq": flip(me, lowest(distance))},
            )
            for which, (source, target) in enumerate(zip(sources, (got, got_lse)))
        ]

    sent = []

    def send(distance):
        for copy in messages(distance):
            copy.start()
            sent.append(copy)

    for distance in sorted(range(1, count, 2), reverse=True):
        send(distance)
    evens = sorted(range(2, count, 2), key=lambda d: (lowest(d), -d))
    for distance in evens + [0]:
        owner = flip(me, distance)
        incoming = [distance | bit for bit in one_bits(lowest(distance) if distance else count)]
        for message in incoming:
            for copy in messages(message):
                copy.wait_recv()
        levels = [mine_lse[distance]] + [got_lse[message] for message in incoming]
        if not distance:
            levels.append(across(tree_lse_ref[...]))
        top = functools.reduce(jnp.maximum, levels)
        shares = [jnp.exp(level - top) for level in levels]
        total = functools.reduce(jnp.add, shares)
        inverse = 1.0 / total
        shares = [jnp.transpose(share * inverse)[:rows] for share in shares]
        if distance:
            held_lse[distance // 2] = top + jnp.log(total)
        for head in range(heads):
            cols = slice(head * 128, (head + 1) * 128)
            pieces = [part_ref[owner, :, cols]] + [got[message, :, cols] for message in incoming]
            if not distance:
                pieces.append(tree_ref[:, cols])
            mixed = functools.reduce(
                jnp.add,
                [
                    piece.astype(jnp.float32) * share[:, head : head + 1]
                    for piece, share in zip(pieces, shares)
                ],
            )
            if distance:
                held[distance // 2, :, cols] = mixed.astype(held.dtype)
            else:
                attended[:, cols] = (mixed * gate_ref[:, head : head + 1]).astype(jnp.bfloat16)
        if distance:
            send(distance)
    load.wait()
    width = out_ref.shape[1]

    def projected(target):
        cols = pl.ds(pl.multiple_of(target * width, 128), width)
        return jnp.dot(attended[...], w_out[:, cols], preferred_element_type=jnp.float32)

    def out_message(hop):
        return pltpu.make_async_remote_copy(
            src_ref=outgoing.at[hop],
            dst_ref=arrived.at[hop],
            send_sem=out_send.at[hop],
            recv_sem=out_recv.at[hop],
            device_id={"kv": (kv + hop) % kv_count},
        )

    for hop in range(1, kv_count):
        outgoing[hop] = projected((kv + hop) % kv_count).astype(jnp.bfloat16)
        copy = out_message(hop)
        copy.start()
        sent.append(copy)
    total = projected(kv)
    for hop in range(1, kv_count):
        out_message(hop).wait_recv()
        total = total + arrived[hop].astype(jnp.float32)
    out_ref[...] = (total + hidden_ref[...].astype(jnp.float32)).astype(jnp.bfloat16)
    for copy in sent:
        copy.wait_send()


def merge_parts(parts, lse, tree_mix, tree_lse, gate, w_out, hidden, count, kv_count):
    rows, width = parts.shape[1:]
    lanes = lse.shape[2]
    half = max(1, count // 2)
    vmem = pl.BlockSpec(memory_space=pltpu.VMEM)
    return pl.pallas_call(
        functools.partial(merge_kernel, count, kv_count),
        out_shape=jax.ShapeDtypeStruct(hidden.shape, jnp.bfloat16),
        in_specs=[vmem] * 5 + [pl.BlockSpec(memory_space=pltpu.HBM), vmem],
        out_specs=vmem,
        scratch_shapes=[
            pltpu.VMEM((count, rows, width), parts.dtype),
            pltpu.VMEM((count, 8, lanes), jnp.float32),
            pltpu.VMEM((count, 8, lanes), jnp.float32),
            pltpu.VMEM((half, rows, width), parts.dtype),
            pltpu.VMEM((half, 8, lanes), jnp.float32),
            pltpu.VMEM(w_out.shape, w_out.dtype),
            pltpu.VMEM((rows, width), jnp.bfloat16),
            pltpu.VMEM((kv_count,) + hidden.shape, jnp.bfloat16),
            pltpu.VMEM((kv_count,) + hidden.shape, jnp.bfloat16),
            pltpu.SemaphoreType.DMA((2, count)),
            pltpu.SemaphoreType.DMA((2, count)),
            pltpu.SemaphoreType.DMA,
            pltpu.SemaphoreType.DMA((kv_count,)),
            pltpu.SemaphoreType.DMA((kv_count,)),
        ],
        compiler_params=pltpu.CompilerParams(
            collective_id=1, has_side_effects=True, vmem_limit_bytes=48 * 2**20
        ),
        name="merge_parts",
    )(parts, lse, tree_mix, tree_lse, gate, w_out, hidden)


def pool_kernel(
    groups,
    per_kv,
    block,
    score_scale,
    prefix_ref,
    own_ref,
    group_ref,
    q_ref,
    k_ref,
    v_ref,
    o_ref,
    lse_ref,
    first_ref,
    last_ref,
    member_ref,
    filled_ref,
):
    requests, tree, width = q_ref.shape
    local_kv = k_ref.shape[1] // 128
    per_group = requests // groups
    base_two = score_scale / math.log(2.0)
    pool_dev = k_ref.shape[0]
    offset = lax.axis_index("seq") * pool_dev

    def place(segment, start, length):
        stop = start + length
        first_ref[segment] = jnp.clip(start - offset, 0, pool_dev)
        last_ref[segment] = jnp.clip(stop - offset, 0, pool_dev)
        return stop

    def place_prefix(group, start):
        filled_ref[group] = 0
        return place(group, start, prefix_ref[group])

    def place_own(owner, start):
        group = group_ref[owner]
        at = filled_ref[group]
        member_ref[group * per_group + at] = owner
        filled_ref[group] = at + 1
        return place(groups + owner, start, own_ref[owner])

    lax.fori_loop(0, requests, place_own, lax.fori_loop(0, groups, place_prefix, 0))
    o_ref[...] = jnp.zeros_like(o_ref)
    lse_ref[...] = jnp.full(lse_ref.shape, NEGATIVE, jnp.float32)

    def attend(owners, first, last):
        count = len(owners) * per_kv * tree
        together = min(local_kv, 2 if len(owners) > 1 else 4)
        for base in range(0, local_kv, together):
            heads = range(base, base + together)
            rows = [
                [(owner, kv * per_kv + sub) for sub in range(per_kv) for owner in owners]
                for kv in heads
            ]
            queries = [
                jnp.concatenate(
                    [q_ref[owner, :, head * 128 : (head + 1) * 128] for owner, head in places], axis=0
                )
                for places in rows
            ]

            def visit(step, carry):
                start = pl.multiple_of(step * block, block)
                slots = start + lax.broadcasted_iota(jnp.int32, (1, block), 1)
                shown = (slots >= first) & (slots < last)
                out = []
                raw = [
                    lax.dot_general(
                        query,
                        k_ref[pl.ds(start, block), kv * 128 : (kv + 1) * 128],
                        (((1,), (1,)), ((), ())),
                        preferred_element_type=jnp.float32,
                    )
                    for kv, query in zip(heads, queries)
                ]
                for kv, scores, (run_max, run_sum, run_num) in zip(heads, raw, carry):
                    scores = jnp.where(shown, scores, NEGATIVE)
                    new_max = jnp.maximum(run_max, jnp.max(scores, axis=1, keepdims=True))
                    weights = jnp.exp2((scores - new_max) * base_two)
                    factor = jnp.exp2((run_max - new_max) * base_two)
                    run_sum = run_sum * factor + jnp.sum(weights, axis=1, keepdims=True)
                    run_num = run_num * factor + jnp.dot(
                        weights.astype(jnp.bfloat16),
                        v_ref[pl.ds(start, block), kv * 128 : (kv + 1) * 128],
                        preferred_element_type=jnp.float32,
                    )
                    out.append((new_max, run_sum, run_num))
                return tuple(out)

            empty = (
                jnp.full((count, 1), NEGATIVE, jnp.float32),
                jnp.zeros((count, 1), jnp.float32),
                jnp.zeros((count, 128), jnp.float32),
            )
            done = lax.fori_loop(
                first // block, (last + block - 1) // block, visit, (empty,) * together
            )
            for places, (run_max, run_sum, run_num) in zip(rows, done):
                mixed = (run_num / run_sum).astype(o_ref.dtype)
                lse = run_max * score_scale + jnp.log(run_sum)
                for place, (owner, head) in enumerate(places):
                    part = slice(place * tree, (place + 1) * tree)
                    o_ref[owner, :, head * 128 : (head + 1) * 128] = mixed[part]
                    lse_ref[owner, :, head : head + 1] = lse[part]

    def group_step(group, unused):
        first, last = first_ref[group], last_ref[group]

        @pl.when(last > first)
        def _():
            attend([member_ref[group * per_group + at] for at in range(per_group)], first, last)

        return unused

    def own_step(owner, unused):
        first, last = first_ref[groups + owner], last_ref[groups + owner]

        @pl.when(last > first)
        def _():
            attend([owner], first, last)

        return unused

    lax.fori_loop(0, groups, group_step, 0)
    lax.fori_loop(0, requests, own_step, 0)


def pool_attention(prefix_len, own_len, request_group, query, keys, values, groups, per_kv, score_scale):
    requests, tree, width = query.shape
    vmem = pl.BlockSpec(memory_space=pltpu.VMEM)
    smem = pl.BlockSpec(memory_space=pltpu.SMEM)
    return pl.pallas_call(
        functools.partial(pool_kernel, groups, per_kv, min(512, keys.shape[0]), score_scale),
        out_shape=(
            jax.ShapeDtypeStruct(query.shape, jnp.bfloat16),
            jax.ShapeDtypeStruct((requests, tree, 128), jnp.float32),
        ),
        in_specs=[smem, smem, smem, vmem, vmem, vmem],
        out_specs=(vmem, vmem),
        scratch_shapes=[
            pltpu.SMEM((groups + requests,), jnp.int32),
            pltpu.SMEM((groups + requests,), jnp.int32),
            pltpu.SMEM((requests,), jnp.int32),
            pltpu.SMEM((groups,), jnp.int32),
        ],
        compiler_params=pltpu.CompilerParams(vmem_limit_bytes=60 * 2**20),
        name="pool_attention",
    )(prefix_len, own_len, request_group, query, keys, values)


def body(
    hidden,
    in_gain,
    w_query,
    key_projection_weight,
    value_projection_weight,
    w_gate,
    w_out,
    q_gain,
    k_gain,
    cache_keys,
    pooled_cache_values,
    prefix_len,
    own_len,
    request_group,
    parents,
    accepted_leaf,
):
    local_req, tree = parents.shape
    groups = prefix_len.shape[0]
    requests = own_len.shape[0]
    head_width = q_gain.shape[0]
    local_heads = w_gate.shape[1]
    local_kv = key_projection_weight.shape[1] // head_width
    per_kv = local_heads // local_kv
    local_tok = hidden.shape[0]
    pool_dev = cache_keys.shape[0]
    seq_index = lax.axis_index("seq")
    score_scale = 1.0 / math.sqrt(head_width)
    seq_count = requests // local_req
    kv_count = in_gain.shape[0] // hidden.shape[1]
    reach, depth_f = tree_paths(parents)
    all_reqs = jnp.arange(requests, dtype=jnp.int32)
    my_reqs = seq_index * local_req + jnp.arange(local_req, dtype=jnp.int32)
    my_pick = (my_reqs[:, None] == all_reqs[None, :]).astype(jnp.int32)
    my_group = jnp.sum(my_pick * request_group[None, :], axis=1)
    group_ids = jnp.arange(groups, dtype=jnp.int32)
    group_pick = (my_group[:, None] == group_ids[None, :]).astype(jnp.int32)
    context = jnp.sum(group_pick * prefix_len[None, :], axis=1) + jnp.sum(
        my_pick * own_len[None, :], axis=1
    )
    positions = (context[:, None].astype(jnp.float32) + depth_f).reshape(-1)
    cosine, sine = rope_tables(positions, head_width)
    seen = (reach[:, :, None, :] * jnp.eye(local_req, dtype=jnp.float32)[:, None, :, None]).reshape(
        local_tok, local_tok
    )
    gathered, key_new, value_new, tree_mix, tree_lse, gate = layer_front(
        hidden,
        in_gain,
        w_query,
        key_projection_weight,
        value_projection_weight,
        w_gate.T,
        q_gain,
        k_gain,
        cosine,
        sine,
        seen,
        seq_count,
        kv_count,
        score_scale,
    )
    parts, part_lse = pool_attention(
        prefix_len,
        own_len,
        request_group,
        gathered.reshape(requests, tree, local_heads * head_width),
        cache_keys.reshape(pool_dev, local_kv * head_width),
        pooled_cache_values.reshape(pool_dev, local_kv * head_width),
        groups,
        per_kv,
        score_scale,
    )
    layer_out = merge_parts(
        parts.reshape(seq_count, local_tok, local_heads * head_width),
        part_lse.reshape(seq_count, local_tok, 128),
        tree_mix,
        tree_lse,
        gate,
        w_out,
        hidden,
        seq_count,
        kv_count,
    )
    tree_rows = jnp.concatenate(
        [
            key_new.reshape(local_req, tree, local_kv * head_width),
            value_new.reshape(local_req, tree, local_kv * head_width),
        ],
        axis=-1,
    )
    picked = accepted_rows(reach, depth_f, accepted_leaf, tree_rows)
    accepted_keys = picked[:, :, : local_kv * head_width]
    accepted_values = picked[:, :, local_kv * head_width :]
    return (layer_out, accepted_keys, accepted_values)


def solution(mesh):
    in_specs = (
        P("seq", "kv"),
        P(),
        P(None, "kv"),
        P(None, "kv"),
        P(None, "kv"),
        P(None, "kv"),
        P("kv", None),
        P(),
        P(),
        P("seq", "kv", None),
        P("seq", "kv", None),
        P(),
        P(),
        P(),
        P("seq", None),
        P("seq"),
    )
    out_specs = (P("seq", "kv"), P("seq", None, "kv"), P("seq", None, "kv"))
    return jax.shard_map(body, mesh=mesh, in_specs=in_specs, out_specs=out_specs, check_vma=False)
```

profile of v0, /device:TPU:0, one launch (start us, length us, event | category | flops | bytes accessed | tf_op | source)
XLA Modules:
  0.0 92.5 jit_solution(11698099213868949067)
XLA Ops:
  0.6 0.7 compare_bitcast_fusion
  1.4 0.9 select_reduce_fusion
  2.3 0.8 fusion.21
  3.2 0.9 %convolution_minimum_fusion.4 = f32[2,32,32]{1,2,0:T(8,128)S(1)} fusion(f32[32,32]{0,1:T(8,128)S(1)} %broadcast_subtract_fusion, s32[2,32]{1,0:T(2,128)} %param.30, f32[32,32]{0,1:T(8,128)S(1)} %fusion.17), kind=kOutput, calls=%fused_computation.7 | convolution fusion | flops 796672 | bytes 16640 | tf_op jit(solution)/shard_map/mij,mjk->mik/dot_general | solution.py:43
  4.1 0.2 convolution_minimum_fusion.3
  4.3 0.2 convolution_minimum_fusion.2
  4.4 0.2 convolution_minimum_fusion.1
  4.6 0.2 fusion.27
  4.8 0.1 fusion.19
  4.9 0.1 copy.23
  5.0 0.1 broadcast_add_fusion
  5.1 0.1 add.57
  5.2 0.1 broadcast_multiply_fusion
  5.3 0.7 mul.100.seen_ref
  6.0 0.2 fusion.18
  6.2 0.7 pad_maximum_fusion
  6.9 0.0 copy-start.6
  6.9 31.1 %layer_front.1 = (bf16[16,64,1024]{2,1,0:T(8,128)(2,1)}, bf16[64,512]{1,0:T(8,128)(2,1)}, bf16[64,512]{1,0:T(8,128)(2,1)}, f32[64,1024]{1,0:T(8,128)}, f32[64,128]{1,0:T(8,128)}, /*index=5*/f32[64,8]{1,0:T(8,128)}) custom-call(bf16[64,1024]{1,0:T(8,128)(2,1)} %hidden_ref.3, f32[1,2048]{1,0:T(1,128)} %bitcast.36, bf16[2048,1024]{1,0:T(8,128)(2,1)} %w_query_ref.1, ...), custom_call_target="tpu_custom_call" | custom-call | tf_op jit(solution)/shard_map/layer_front/pallas_call | solution.py:277
  38.1 1.3 %convolution_convert_fusion = bf16[2,32,1024]{2,1,0:T(8,128)(2,1)S(1)} fusion(bf16[2,32,512]{2,1,0:T(8,128)(2,1)} %bitcast.34, bf16[2,32,512]{2,1,0:T(8,128)(2,1)} %bitcast.33, f32[2,32]{1,0:T(2,128)S(1)} %bitcast.37, f32[32]{0:T(128)S(1)} %iota_convert_fusion, f32[2,32]{1,0:T(2,128)S(1)} %get-tuple-element.23), kind=kOutput, calls=%fused_computation.2 | convolution fusion | flops 25497600 | bytes 262784 | tf_op jit(solution)/shard_map/mdj,mjc->mdc/dot_general | solution.py:56
  39.3 0.7 fusion.26
  40.0 0.0 copy-done.6
  40.0 4.3 %copy_bitcast_fusion = (bf16[2048,512]{1,0:T(8,128)(2,1)}, bf16[2048,512]{1,0:T(8,128)(2,1)}) fusion(bf16[256,8,4,128]{3,2,1,0:T(4,128)(2,1)S(1)} %bitcast.31, bf16[256,8,4,128]{3,2,1,0:T(4,128)(2,1)} %bitcast.32), kind=kLoop, calls=%fused_computation | loop fusion | bytes 8388608 | tf_op jit(solution)/shard_map/reshape | solution.py:695
  44.2 0.0 copy-start.1
  44.2 0.0 copy-start.3
  44.2 0.0 copy-start.4
  44.2 0.0 copy-start.5
  44.2 16.2 %pool_attention.1 = (bf16[32,32,1024]{2,1,0:T(8,128)(2,1)}, f32[32,32,128]{2,1,0:T(8,128)}) custom-call(s32[4]{0:T(128)} %prefix_ref.1, s32[32]{0:T(128)} %own_ref.1, s32[32]{0:T(128)} %group_ref.1, bf16[32,32,1024]{2,1,0:T(8,128)(2,1)} %bitcast.30, bf16[2048,512]{1,0:T(8,128)(2,1)} %get-tuple-element.33.k_ref, bf16[2048,512]{1,0:T(8,128)(2,1)} %get-tuple-element.32.v_ref), custom_call_target="tpu_custom_call" | custom-call | tf_op jit(solution)/shard_map/pool_attention/pallas_call | solution.py:608
  60.4 0.0 copy-done.1
  60.4 0.0 copy-done.3
  60.4 0.0 copy-done.4
  60.4 0.0 copy-done.5
  60.4 0.0 copy-start
  60.4 1.6 %copy-done = bf16[32,32,1024]{2,1,0:T(8,128)(2,1)S(1)} copy-done((bf16[32,32,1024]{2,1,0:T(8,128)(2,1)S(1)}, bf16[32,32,1024]{2,1,0:T(8,128)(2,1)}, u32[]{:S(2)}) %copy-start) | copy-done | bytes 2097176
  62.0 0.0 copy-start.2
  62.0 1.0 %copy-done.2 = f32[32,32,128]{2,1,0:T(8,128)S(1)} copy-done((f32[32,32,128]{2,1,0:T(8,128)S(1)}, f32[32,32,128]{2,1,0:T(8,128)}, u32[]{:S(2)}) %copy-start.2) | copy-done | bytes 524312
  63.1 28.8 %merge_parts.1 = bf16[64,1024]{1,0:T(8,128)(2,1)S(1)} custom-call(bf16[16,64,1024]{2,1,0:T(8,128)(2,1)S(1)} %bitcast.28, f32[16,64,128]{2,1,0:T(8,128)S(1)} %bitcast.29, f32[64,1024]{1,0:T(8,128)S(1)} %copy-done.3, f32[64,128]{1,0:T(8,128)S(1)} %copy-done.4, f32[64,8]{1,0:T(8,128)S(1)} %copy-done.5, bf16[1024,2048]{1,0:T(8,128)(2,1)} %w_out_ref.1, ...), custom_call_target="tpu_custom_call" | custom-call | tf_op jit(solution)/shard_map/merge_parts/pallas_call | solution.py:448
  91.9 0.7 copy.36
  (7 shorter events, 0.0 us)
Async XLA Ops:
  6.9 33.1 %copy-start.6 = (bf16[2048,4,128]{2,1,0:T(4,128)(2,1)S(1)}, bf16[2048,4,128]{2,1,0:T(4,128)(2,1)}, u32[]{:S(2)}) copy-start(bf16[2048,4,128]{2,1,0:T(4,128)(2,1)} %param.26) | copy-start | bytes 6291460
  44.2 16.2 %copy-start.1 = (bf16[64,1024]{1,0:T(8,128)(2,1)S(1)}, bf16[64,1024]{1,0:T(8,128)(2,1)}, u32[]{:S(2)}) copy-start(bf16[64,1024]{1,0:T(8,128)(2,1)} %hidden_ref.3) | copy-start | bytes 393220
  44.2 16.2 %copy-start.3 = (f32[64,1024]{1,0:T(8,128)S(1)}, f32[64,1024]{1,0:T(8,128)}, u32[]{:S(2)}) copy-start(f32[64,1024]{1,0:T(8,128)} %get-tuple-element.14.tree_ref) | copy-start | bytes 786436
  44.2 16.2 %copy-start.4 = (f32[64,128]{1,0:T(8,128)S(1)}, f32[64,128]{1,0:T(8,128)}, u32[]{:S(2)}) copy-start(f32[64,128]{1,0:T(8,128)} %get-tuple-element.15.tree_lse_ref) | copy-start | bytes 98308
  44.2 16.2 %copy-start.5 = (f32[64,8]{1,0:T(8,128)S(1)}, f32[64,8]{1,0:T(8,128)}, u32[]{:S(2)}) copy-start(f32[64,8]{1,0:T(8,128)} %get-tuple-element.16.gate_ref) | copy-start | bytes 6148
  60.4 1.6 %copy-start = (bf16[32,32,1024]{2,1,0:T(8,128)(2,1)S(1)}, bf16[32,32,1024]{2,1,0:T(8,128)(2,1)}, u32[]{:S(2)}) copy-start(bf16[32,32,1024]{2,1,0:T(8,128)(2,1)} %get-tuple-element.12) | copy-start | bytes 6291460
  62.0 1.0 %copy-start.2 = (f32[32,32,128]{2,1,0:T(8,128)S(1)}, f32[32,32,128]{2,1,0:T(8,128)}, u32[]{:S(2)}) copy-start(f32[32,32,128]{2,1,0:T(8,128)} %get-tuple-element.13) | copy-start | bytes 1572868
where the time goes:
time: 92.6 us; the launch traced here: 92.5 us
  Pallas kernels  76.1 us (82%)
  local copies, waits for them, and re-layouts  9.09 us (10%)
  other arithmetic  3.58 us (4%)
  matrix products  2.99 us (3%)
    pallas_call x1, Pallas kernels, layer_front(): pl.pallas_call(functools.partial(layer_kernel, count, kv_count, score_sca...  31.1 us
    pallas_call x1, Pallas kernels, merge_parts(): pl.pallas_call(functools.partial(merge_kernel, count, kv_count), out_shap...  28.8 us
    pallas_call x1, Pallas kernels, pool_attention(): pl.pallas_call(functools.partial(pool_kernel, groups, per_kv, min(512, ke...  16.2 us
    reshape x1, local copies, waits for them, and re-layouts, body(): pooled_cache_values.reshape(pool_dev, local_kv * head_width)  4.25 us
    unnamed x15, local copies, waits for them, and re-layouts  3.3 us

commit v1 on v0

--- a/solution.py
+++ b/solution.py
@@ -478,9 +478,7 @@
     per_kv,
     block,
     score_scale,
-    prefix_ref,
-    own_ref,
-    group_ref,
+    facts_ref,
     q_ref,
     k_ref,
     v_ref,
@@ -506,14 +504,14 @@
 
     def place_prefix(group, start):
         filled_ref[group] = 0
-        return place(group, start, prefix_ref[group])
+        return place(group, start, facts_ref[group])
 
     def place_own(owner, start):
-        group = group_ref[owner]
+        group = facts_ref[groups + requests + owner]
         at = filled_ref[group]
         member_ref[group * per_group + at] = owner
         filled_ref[group] = at + 1
-        return place(groups + owner, start, own_ref[owner])
+        return place(groups + owner, start, facts_ref[groups + owner])
 
     lax.fori_loop(0, requests, place_own, lax.fori_loop(0, groups, place_prefix, 0))
     o_ref[...] = jnp.zeros_like(o_ref)
@@ -601,7 +599,7 @@
     lax.fori_loop(0, requests, own_step, 0)
 
 
-def pool_attention(prefix_len, own_len, request_group, query, keys, values, groups, per_kv, score_scale):
+def pool_attention(facts, query, keys, values, groups, per_kv, score_scale):
     requests, tree, width = query.shape
     vmem = pl.BlockSpec(memory_space=pltpu.VMEM)
     smem = pl.BlockSpec(memory_space=pltpu.SMEM)
@@ -611,7 +609,7 @@
             jax.ShapeDtypeStruct(query.shape, jnp.bfloat16),
             jax.ShapeDtypeStruct((requests, tree, 128), jnp.float32),
         ),
-        in_specs=[smem, smem, smem, vmem, vmem, vmem],
+        in_specs=[smem, vmem, vmem, vmem],
         out_specs=(vmem, vmem),
         scratch_shapes=[
             pltpu.SMEM((groups + requests,), jnp.int32),
@@ -619,9 +617,9 @@
             pltpu.SMEM((requests,), jnp.int32),
             pltpu.SMEM((groups,), jnp.int32),
         ],
-        compiler_params=pltpu.CompilerParams(vmem_limit_bytes=60 * 2**20),
+        compiler_params=pltpu.CompilerParams(vmem_limit_bytes=48 * 2**20),
         name="pool_attention",
-    )(prefix_len, own_len, request_group, query, keys, values)
+    )(facts, query, keys, values)
 
 
 def body(
@@ -687,9 +685,7 @@
         score_scale,
     )
     parts, part_lse = pool_attention(
-        prefix_len,
-        own_len,
-        request_group,
+        jnp.concatenate([prefix_len, own_len, request_group]),
         gathered.reshape(requests, tree, local_heads * head_width),
         cache_keys.reshape(pool_dev, local_kv * head_width),
         pooled_cache_values.reshape(pool_dev, local_kv * head_width),

time: 92.6 us -> 90.5 us (0.977)
  local copies, waits for them, and re-layouts: 9.09 us -> 6.73 us
    unnamed x15 -> x13, local copies, waits for them, and re-layouts: 3.3 us -> 0.68 us
    pallas_call x1, Pallas kernels: 16.2 us -> 15.2 us  [pool_attention(): pl.pallas_call(functools.partial(pool_kernel, groups, per_kv, min(512, ke...]
where the time goes in v1:
time: 90.5 us; the launch traced here: 90.3 us
  Pallas kernels  75.4 us (83%)
  local copies, waits for them, and re-layouts  6.73 us (7%)
  other arithmetic  4.35 us (5%)
  matrix products  2.99 us (3%)
    pallas_call x1, Pallas kernels, layer_front(): pl.pallas_call(functools.partial(layer_kernel, count, kv_count, score_sca...  31.2 us
    pallas_call x1, Pallas kernels, merge_parts(): pl.pallas_call(functools.partial(merge_kernel, count, kv_count), out_shap...  29.1 us
    pallas_call x1, Pallas kernels, pool_attention(): pl.pallas_call(functools.partial(pool_kernel, groups, per_kv, min(512, ke...  15.2 us
    reshape x1, local copies, waits for them, and re-layouts, body(): pooled_cache_values.reshape(pool_dev, local_kv * head_width)  4.51 us

profile of v1, /device:TPU:0, one launch (start us, length us, event | category | flops | bytes accessed | tf_op | source)
XLA Modules:
  0.0 90.3 jit_solution(18308953686354962860)
XLA Ops:
  0.6 0.7 compare_bitcast_fusion
  1.4 0.8 pad_add_fusion.facts_ref
  2.2 0.9 select_reduce_fusion
  3.0 0.8 fusion.21
  3.9 0.9 %convolution_minimum_fusion.4 = f32[2,32,32]{1,2,0:T(8,128)S(1)} fusion(f32[32,32]{0,1:T(8,128)S(1)} %broadcast_subtract_fusion, s32[2,32]{1,0:T(2,128)} %param.30, f32[32,32]{0,1:T(8,128)S(1)} %fusion.17), kind=kOutput, calls=%fused_computation.7 | convolution fusion | flops 796672 | bytes 16640 | tf_op jit(solution)/shard_map/mij,mjk->mik/dot_general | solution.py:43
  4.9 0.2 convolution_minimum_fusion.3
  5.0 0.2 convolution_minimum_fusion.2
  5.2 0.2 convolution_minimum_fusion.1
  5.4 0.2 fusion.27
  5.6 0.1 fusion.19
  5.7 0.1 copy.23
  5.8 0.1 broadcast_add_fusion
  5.8 0.1 add.57
  5.9 0.1 broadcast_multiply_fusion
  6.0 0.7 mul.100.seen_ref
  6.8 0.2 fusion.18
  7.0 0.7 pad_maximum_fusion
  7.7 0.0 copy-start.5
  7.7 31.2 %layer_front.1 = (bf16[16,64,1024]{2,1,0:T(8,128)(2,1)}, bf16[64,512]{1,0:T(8,128)(2,1)}, bf16[64,512]{1,0:T(8,128)(2,1)}, f32[64,1024]{1,0:T(8,128)}, f32[64,128]{1,0:T(8,128)}, /*index=5*/f32[64,8]{1,0:T(8,128)}) custom-call(bf16[64,1024]{1,0:T(8,128)(2,1)} %hidden_ref.3, f32[1,2048]{1,0:T(1,128)} %bitcast.36, bf16[2048,1024]{1,0:T(8,128)(2,1)} %w_query_ref.1, ...), custom_call_target="tpu_custom_call" | custom-call | tf_op jit(solution)/shard_map/layer_front/pallas_call | solution.py:277
  38.9 1.3 %convolution_convert_fusion = bf16[2,32,1024]{2,1,0:T(8,128)(2,1)S(1)} fusion(bf16[2,32,512]{2,1,0:T(8,128)(2,1)} %bitcast.34, bf16[2,32,512]{2,1,0:T(8,128)(2,1)} %bitcast.33, f32[2,32]{1,0:T(2,128)S(1)} %bitcast.37, f32[32]{0:T(128)S(1)} %iota_convert_fusion, f32[2,32]{1,0:T(2,128)S(1)} %get-tuple-element.23), kind=kOutput, calls=%fused_computation.2 | convolution fusion | flops 25497600 | bytes 262784 | tf_op jit(solution)/shard_map/mdj,mjc->mdc/dot_general | solution.py:56
  40.1 0.7 fusion.26
  40.8 0.0 copy-done.5
  40.8 0.0 copy-start
  40.8 4.5 %copy_bitcast_fusion = (bf16[2048,512]{1,0:T(8,128)(2,1)}, bf16[2048,512]{1,0:T(8,128)(2,1)}) fusion(bf16[256,8,4,128]{3,2,1,0:T(4,128)(2,1)S(1)} %bitcast.31, bf16[256,8,4,128]{3,2,1,0:T(4,128)(2,1)} %bitcast.32), kind=kLoop, calls=%fused_computation | loop fusion | bytes 8388608 | tf_op jit(solution)/shard_map/reshape | solution.py:691
  45.3 0.0 copy-done
  45.3 0.0 copy-start.1
  45.3 0.0 copy-start.2
  45.3 0.0 copy-start.3
  45.3 0.0 copy-start.4
  45.3 15.2 %pool_attention.1 = (bf16[32,32,1024]{2,1,0:T(8,128)(2,1)S(1)}, f32[32,32,128]{2,1,0:T(8,128)S(1)}) custom-call(s32[68]{0:T(128)S(1)} %pad_add_fusion.facts_ref, bf16[32,32,1024]{2,1,0:T(8,128)(2,1)S(1)} %bitcast.28, bf16[2048,512]{1,0:T(8,128)(2,1)} %get-tuple-element.33.k_ref, bf16[2048,512]{1,0:T(8,128)(2,1)} %get-tuple-element.32.v_ref), custom_call_target="tpu_custom_call" | custom-call | tf_op jit(solution)/shard_map/pool_attention/pallas_call | solution.py:606
  60.5 0.0 copy-done.1
  60.5 0.0 copy-done.2
  60.5 0.0 copy-done.3
  60.5 0.0 copy-done.4
  60.6 29.1 %merge_parts.1 = bf16[64,1024]{1,0:T(8,128)(2,1)S(1)} custom-call(bf16[16,64,1024]{2,1,0:T(8,128)(2,1)S(1)} %bitcast.29, f32[16,64,128]{2,1,0:T(8,128)S(1)} %bitcast.30, f32[64,1024]{1,0:T(8,128)S(1)} %copy-done.2, f32[64,128]{1,0:T(8,128)S(1)} %copy-done.3, f32[64,8]{1,0:T(8,128)S(1)} %copy-done.4, bf16[1024,2048]{1,0:T(8,128)(2,1)} %w_out_ref.1, ...), custom_call_target="tpu_custom_call" | custom-call | tf_op jit(solution)/shard_map/merge_parts/pallas_call | solution.py:448
  89.6 0.7 copy.36
  (7 shorter events, 0.0 us)
Async XLA Ops:
  7.7 33.1 %copy-start.5 = (bf16[2048,4,128]{2,1,0:T(4,128)(2,1)S(1)}, bf16[2048,4,128]{2,1,0:T(4,128)(2,1)}, u32[]{:S(2)}) copy-start(bf16[2048,4,128]{2,1,0:T(4,128)(2,1)} %param.26) | copy-start | bytes 6291460
  40.8 4.5 %copy-start = (bf16[16,64,1024]{2,1,0:T(8,128)(2,1)S(1)}, bf16[16,64,1024]{2,1,0:T(8,128)(2,1)}, u32[]{:S(2)}) copy-start(bf16[16,64,1024]{2,1,0:T(8,128)(2,1)} %get-tuple-element.11) | copy-start | bytes 6291460
  45.3 15.2 %copy-start.1 = (bf16[64,1024]{1,0:T(8,128)(2,1)S(1)}, bf16[64,1024]{1,0:T(8,128)(2,1)}, u32[]{:S(2)}) copy-start(bf16[64,1024]{1,0:T(8,128)(2,1)} %hidden_ref.3) | copy-start | bytes 393220
  45.3 15.2 %copy-start.2 = (f32[64,1024]{1,0:T(8,128)S(1)}, f32[64,1024]{1,0:T(8,128)}, u32[]{:S(2)}) copy-start(f32[64,1024]{1,0:T(8,128)} %get-tuple-element.14.tree_ref) | copy-start | bytes 786436
  45.3 15.2 %copy-start.3 = (f32[64,128]{1,0:T(8,128)S(1)}, f32[64,128]{1,0:T(8,128)}, u32[]{:S(2)}) copy-start(f32[64,128]{1,0:T(8,128)} %get-tuple-element.15.tree_lse_ref) | copy-start | bytes 98308
  45.3 15.2 %copy-start.4 = (f32[64,8]{1,0:T(8,128)S(1)}, f32[64,8]{1,0:T(8,128)}, u32[]{:S(2)}) copy-start(f32[64,8]{1,0:T(8,128)} %get-tuple-element.16.gate_ref) | copy-start | bytes 6148

commit v2 on v1

--- a/solution.py
+++ b/solution.py
@@ -467,7 +467,7 @@
             pltpu.SemaphoreType.DMA((kv_count,)),
         ],
         compiler_params=pltpu.CompilerParams(
-            collective_id=1, has_side_effects=True, vmem_limit_bytes=48 * 2**20
+            collective_id=1, has_side_effects=True, vmem_limit_bytes=60 * 2**20
         ),
         name="merge_parts",
     )(parts, lse, tree_mix, tree_lse, gate, w_out, hidden)

time: 90.5 us -> 95.9 us (1.060)
  local copies, waits for them, and re-layouts: 6.73 us -> 9.76 us
  Pallas kernels: 75.4 us -> 77.8 us
    unnamed x13 -> x9, local copies, waits for them, and re-layouts: 0.68 us -> 3.7 us
    pallas_call x1, Pallas kernels: 29.1 us -> 31.5 us  [merge_parts(): pl.pallas_call(functools.partial(merge_kernel, count, kv_count), out_shap...]
where the time goes in v2:
time: 95.9 us; the launch traced here: 95.7 us
  Pallas kernels  77.8 us (81%)
  local copies, waits for them, and re-layouts  9.76 us (10%)
  other arithmetic  4.35 us (5%)
  matrix products  2.99 us (3%)
    pallas_call x1, Pallas kernels, merge_parts(): pl.pallas_call(functools.partial(merge_kernel, count, kv_count), out_shap...  31.5 us
    pallas_call x1, Pallas kernels, layer_front(): pl.pallas_call(functools.partial(layer_kernel, count, kv_count, score_sca...  31.2 us
    pallas_call x1, Pallas kernels, pool_attention(): pl.pallas_call(functools.partial(pool_kernel, groups, per_kv, min(512, ke...  15.1 us
    reshape x1, local copies, waits for them, and re-layouts, body(): pooled_cache_values.reshape(pool_dev, local_kv * head_width)  4.52 us
    unnamed x9, local copies, waits for them, and re-layouts  3.7 us

profile of v2, /device:TPU:0, one launch (start us, length us, event | category | flops | bytes accessed | tf_op | source)
XLA Modules:
  0.0 95.7 jit_solution(3747355893792474371)
XLA Ops:
  0.6 0.7 compare_bitcast_fusion
  1.4 0.8 pad_add_fusion.facts_ref
  2.2 0.9 select_reduce_fusion
  3.0 0.8 fusion.21
  3.9 0.9 convolution_minimum_fusion.4
  4.9 0.2 convolution_minimum_fusion.3
  5.0 0.2 convolution_minimum_fusion.2
  5.2 0.2 convolution_minimum_fusion.1
  5.4 0.2 fusion.27
  5.6 0.1 fusion.19
  5.7 0.1 copy.23
  5.8 0.1 broadcast_add_fusion
  5.8 0.1 add.57
  5.9 0.1 broadcast_multiply_fusion
  6.0 0.7 mul.100.seen_ref
  6.8 0.2 fusion.18
  7.0 0.7 pad_maximum_fusion
  7.7 0.0 copy-start.3
  7.7 31.2 %layer_front.1 = (bf16[16,64,1024]{2,1,0:T(8,128)(2,1)}, bf16[64,512]{1,0:T(8,128)(2,1)}, bf16[64,512]{1,0:T(8,128)(2,1)}, f32[64,1024]{1,0:T(8,128)}, f32[64,128]{1,0:T(8,128)}, /*index=5*/f32[64,8]{1,0:T(8,128)}) custom-call(bf16[64,1024]{1,0:T(8,128)(2,1)} %hidden_ref.3, f32[1,2048]{1,0:T(1,128)} %bitcast.36, bf16[2048,1024]{1,0:T(8,128)(2,1)} %w_query_ref.1, ...), custom_call_target="tpu_custom_call" | custom-call | tf_op jit(solution)/shard_map/layer_front/pallas_call | solution.py:277
  38.9 1.3 %convolution_convert_fusion = bf16[2,32,1024]{2,1,0:T(8,128)(2,1)S(1)} fusion(bf16[2,32,512]{2,1,0:T(8,128)(2,1)} %bitcast.34, bf16[2,32,512]{2,1,0:T(8,128)(2,1)} %bitcast.33, f32[2,32]{1,0:T(2,128)S(1)} %bitcast.37, f32[32]{0:T(128)S(1)} %iota_convert_fusion, f32[2,32]{1,0:T(2,128)S(1)} %get-tuple-element.23), kind=kOutput, calls=%fused_computation.2 | convolution fusion | flops 25497600 | bytes 262784 | tf_op jit(solution)/shard_map/mdj,mjc->mdc/dot_general | solution.py:56
  40.2 0.7 fusion.26
  40.8 0.0 copy-done.3
  40.8 0.0 copy-start
  40.8 4.5 %copy_bitcast_fusion = (bf16[2048,512]{1,0:T(8,128)(2,1)}, bf16[2048,512]{1,0:T(8,128)(2,1)}) fusion(bf16[256,8,4,128]{3,2,1,0:T(4,128)(2,1)S(1)} %bitcast.31, bf16[256,8,4,128]{3,2,1,0:T(4,128)(2,1)} %bitcast.32), kind=kLoop, calls=%fused_computation | loop fusion | bytes 8388608 | tf_op jit(solution)/shard_map/reshape | solution.py:691
  45.3 0.0 copy-done
  45.3 15.1 %pool_attention.1 = (bf16[32,32,1024]{2,1,0:T(8,128)(2,1)S(1)}, f32[32,32,128]{2,1,0:T(8,128)S(1)}) custom-call(s32[68]{0:T(128)S(1)} %pad_add_fusion.facts_ref, bf16[32,32,1024]{2,1,0:T(8,128)(2,1)S(1)} %bitcast.28, bf16[2048,512]{1,0:T(8,128)(2,1)} %get-tuple-element.33.k_ref, bf16[2048,512]{1,0:T(8,128)(2,1)} %get-tuple-element.32.v_ref), custom_call_target="tpu_custom_call" | custom-call | tf_op jit(solution)/shard_map/pool_attention/pallas_call | solution.py:606
  60.5 0.0 copy-start.1
  60.5 1.3 %copy-done.1 = bf16[32,32,1024]{2,1,0:T(8,128)(2,1)} copy-done((bf16[32,32,1024]{2,1,0:T(8,128)(2,1)}, bf16[32,32,1024]{2,1,0:T(8,128)(2,1)S(1)}, u32[]{:S(2)}) %copy-start.1) | copy-done | bytes 2097176
  61.8 0.0 copy-start.2
  61.8 0.8 copy-done.2
  62.6 31.5 %merge_parts.1 = bf16[64,1024]{1,0:T(8,128)(2,1)} custom-call(bf16[16,64,1024]{2,1,0:T(8,128)(2,1)} %bitcast.29, f32[16,64,128]{2,1,0:T(8,128)} %bitcast.30, f32[64,1024]{1,0:T(8,128)} %get-tuple-element.14.tree_ref, f32[64,128]{1,0:T(8,128)} %get-tuple-element.15.tree_lse_ref, f32[64,8]{1,0:T(8,128)} %get-tuple-element.16.gate_ref, ...), custom_call_target="tpu_custom_call" | custom-call | tf_op jit(solution)/shard_map/merge_parts/pallas_call | solution.py:448
  94.1 1.6 %copy.36 = bf16[64,1024]{1,0:T(8,128)(2,1)} copy(bf16[64,1024]{1,0:T(8,128)(2,1)} %merge_parts.1) | data formatting | bytes 262144
  (7 shorter events, 0.0 us)
Async XLA Ops:
  7.7 33.1 %copy-start.3 = (bf16[2048,4,128]{2,1,0:T(4,128)(2,1)S(1)}, bf16[2048,4,128]{2,1,0:T(4,128)(2,1)}, u32[]{:S(2)}) copy-start(bf16[2048,4,128]{2,1,0:T(4,128)(2,1)} %param.26) | copy-start | bytes 6291460
  40.8 4.5 %copy-start = (bf16[16,64,1024]{2,1,0:T(8,128)(2,1)S(1)}, bf16[16,64,1024]{2,1,0:T(8,128)(2,1)}, u32[]{:S(2)}) copy-start(bf16[16,64,1024]{2,1,0:T(8,128)(2,1)} %get-tuple-element.11) | copy-start | bytes 6291460
  60.5 1.3 %copy-start.1 = (bf16[32,32,1024]{2,1,0:T(8,128)(2,1)}, bf16[32,32,1024]{2,1,0:T(8,128)(2,1)S(1)}, u32[]{:S(2)}) copy-start(bf16[32,32,1024]{2,1,0:T(8,128)(2,1)S(1)} %get-tuple-element.12) | copy-start | bytes 6291460
  61.8 0.8 copy-start.2
